TPU v7x, 32 devices: a whole 2x2x4 slice. The times are simulated.
32 devices in a mesh: dp: 4 (over y, x), block: 8 (over z, core).
Axes of the slice: x: 2, y: 2, z: 4, core: 2. Of those that a mesh axis runs over, the one named last changes fastest.
Arguments:
- positions: float32 [3, 8192], P(None, ('dp', 'block')), may hold values from -4 to 4
- neighbours: int32 [16, 8192], P(None, ('dp', 'block')), may hold values from 0 to 32
- atom_species: int32 [8192], P(('dp', 'block')), may hold values from 0 to 3
- tagged_atom: int32 [256], P(('dp', 'block')), may hold values from 0 to 31
- observed_in: int32 [256], P(('dp', 'block')), may hold values from 0 to 15
- targets: float32 [64], replicated, may hold values from -3 to 3
- noise_level: float32 [64], replicated, may hold values from 0.1 to 1
- embed_scale: float32 [4, 128], replicated, may hold values from -4 to 4
- embed_shift: float32 [4, 128], replicated, may hold values from -3 to 3
- first_weight: float32 [128, 256], replicated, may hold values from -1.5 to 1.5
- first_bias: float32 [256], replicated, may hold values from -3 to 3
- middle_weight: float32 [256, 256], replicated, may hold values from -0.375 to 0.375
- middle_bias: float32 [256], replicated, may hold values from -3 to 3
- energy_weight: float32 [4, 256], replicated, may hold values from -0.375 to 0.375
- covariance: float32 [8, 2048, 2048], P('block', 'dp'), as said below
Outputs:
- new_weights: float32 [8, 2048], P('block', 'dp')
- new_covariance: float32 [8, 2048, 2048], P('block', 'dp')
Inputs may be any that keep to these rules, and one draw needn't show every extreme that they name: `neighbours`: a value of 32 marks an empty slot; any other value counts an atom of the same structure. `tagged_atom`: counted within the structure. `observed_in`: the observation is counted within the structure's group. `covariance`: every block is symmetric and positive definite.
All inputs are finite; a program needn't handle non-finite values.
Results may differ from a plain program's by a relative error of at most 0.0003.
Values sent between devices are 32-bit elements; how exact they have to be, the bound alone decides.
A program may use at most 64 MiB of HBM per device.

v0:
```python
import jax
import jax.numpy as jnp
import numpy as np
from jax import lax
from jax.sharding import PartitionSpec as P

OBS = 64


radial_width = 4.0
forgetting = 0.98
highest = lax.Precision.HIGHEST


def observations(
    window,
    positions,
    neighbours,
    atom_species,
    tagged_atom,
    observed_in,
    embed_scale,
    embed_shift,
    first_weight,
    first_bias,
    middle_weight,
    middle_bias,
    energy_weight,
    obs_count,
    weighting,
):
    atom_total = positions.shape[1]
    struct_total = tagged_atom.shape[0]
    struct_size = atom_total // struct_total
    species_count = embed_scale.shape[0]
    slot_count = neighbours.shape[0]
    struct_start = jnp.arange(atom_total, dtype=jnp.int32) // struct_size * struct_size
    live_slot = (neighbours < struct_size).astype(jnp.float32)
    neighbour_at = struct_start[None, :] + jnp.minimum(neighbours, struct_size - 1)
    near_species = atom_species[neighbour_at]
    species_range = jnp.arange(species_count, dtype=jnp.int32)
    species_table = (near_species[None, :, :] == species_range[:, None, None]).astype(jnp.float32)
    edge_scale = jnp.einsum("se,ska->eka", embed_scale, species_table, precision=highest)
    edge_shift = jnp.einsum("se,ska->eka", embed_shift, species_table, precision=highest)
    own_species = (atom_species[None, :] == species_range[:, None]).astype(jnp.float32)
    readout = jnp.dot(energy_weight.T, own_species, precision=highest)
    remainder = middle_weight[window.shape[0] :]

    def site_energy(coords, middle):
        displace = coords[:, neighbour_at] - coords[:, None, :]
        distance_sq = jnp.sum(displace * displace, axis=0)
        radial = jnp.exp(-distance_sq / radial_width) * live_slot
        embedded = jnp.tanh(radial[None] * edge_scale + edge_shift)
        descriptor = jnp.sum(radial[None] * embedded, axis=1) / slot_count
        first_layer = jnp.tanh(
            jnp.dot(first_weight.T, descriptor, precision=highest) + first_bias[:, None]
        )
        second_layer = jnp.tanh(
            jnp.dot(middle.T, first_layer, precision=highest) + middle_bias[:, None]
        )
        return jnp.sum(readout * second_layer, axis=0)

    def predict(window_part):
        middle = jnp.concatenate([window_part, remainder], axis=0)
        energies, pullback = jax.vjp(lambda coords: site_energy(coords, middle), positions)
        forces = -pullback(jnp.ones_like(energies))[0]
        per_struct = jnp.sum(energies.reshape(struct_total, struct_size), axis=1) / struct_size
        tag_table = (
            tagged_atom[:, None] == jnp.arange(struct_size, dtype=jnp.int32)[None, :]
        ).astype(jnp.float32)
        picked = jnp.sum(forces.reshape(3, struct_total, struct_size) * tag_table[None], axis=2)
        values = jnp.concatenate([per_struct[None, :], picked], axis=0)
        value_rows = values[np.arange(obs_count) % 4]
        chosen = (observed_in[None, :] == jnp.arange(obs_count, dtype=jnp.int32)[:, None]).astype(
            jnp.float32
        )
        return jnp.sum(chosen * value_rows, axis=1) * weighting

    predicted, pullback = jax.vjp(predict, window)
    basis = jnp.eye(obs_count, dtype=predicted.dtype)
    jacobian = lax.map(lambda row: pullback(row)[0], basis)
    return (predicted, jacobian)


def local(
    positions,
    neighbours,
    atom_species,
    tagged_atom,
    observed_in,
    targets,
    noise_level,
    embed_scale,
    embed_shift,
    first_weight,
    first_bias,
    middle_weight,
    middle_bias,
    energy_weight,
    covariance,
):
    group_count = lax.axis_size("dp")
    block_count = lax.axis_size("block")
    block_order = covariance.shape[2]
    row_share = covariance.shape[1]
    hidden = middle_weight.shape[1]
    block_rows = block_order // hidden
    window = middle_weight[: block_rows * block_count]
    obs_group = OBS // group_count
    weighting = OBS / (tagged_atom.shape[0] * group_count * block_count)
    predicted_here, jacobian_here = observations(
        window,
        positions,
        neighbours,
        atom_species,
        tagged_atom,
        observed_in,
        embed_scale,
        embed_shift,
        first_weight,
        first_bias,
        middle_weight,
        middle_bias,
        energy_weight,
        obs_group,
        weighting,
    )
    spread = jnp.zeros((OBS,), jnp.float32)
    spread = lax.dynamic_update_slice_in_dim(
        spread, predicted_here, lax.axis_index("dp") * obs_group, 0
    )
    predicted = lax.psum(spread, ("dp", "block"))
    jacobian_block = lax.psum_scatter(jacobian_here, "block", scatter_dimension=1, tiled=True)
    jacobian = lax.all_gather(
        jacobian_block.reshape(obs_group, block_order), "dp", axis=0, tiled=True
    )
    cov_rows = covariance[0]
    product = jnp.dot(cov_rows, jacobian.T, precision=highest)
    columns = lax.dynamic_slice_in_dim(jacobian, lax.axis_index("dp") * row_share, row_share, 1)
    partial_value = jnp.dot(columns, product, precision=highest)
    gram_sum = lax.psum(partial_value, ("dp", "block"))
    gram_sum = 0.5 * (gram_sum + gram_sum.T) + jnp.diag(noise_level)
    factor = jnp.linalg.cholesky(gram_sum)
    inverse = jax.scipy.linalg.cho_solve((factor, True), jnp.eye(OBS, dtype=jnp.float32))
    gain_rows = jnp.dot(product, inverse, precision=highest)
    gains_all = lax.all_gather(gain_rows, "dp", axis=0, tiled=True)
    update = jnp.dot(product, gains_all.T, precision=highest)
    innovation = targets - predicted
    block_window = lax.dynamic_slice_in_dim(
        window.reshape(block_count, block_order), lax.axis_index("block"), 1, 0
    )
    window_rows = lax.dynamic_slice_in_dim(
        block_window, lax.axis_index("dp") * row_share, row_share, 1
    )
    new_weights = window_rows + jnp.dot(gain_rows, innovation, precision=highest)[None, :]
    new_covariance = ((cov_rows - update) / forgetting)[None]
    return (new_weights, new_covariance)


def solution(mesh):
    return jax.shard_map(
        local,
        mesh=mesh,
        in_specs=(
            P(None, ("dp", "block")),
            P(None, ("dp", "block")),
            P(("dp", "block")),
            P(("dp", "block")),
            P(("dp", "block")),
            P(),
            P(),
            P(),
            P(),
            P(),
            P(),
            P(),
            P(),
            P(),
            P("block", "dp", None),
        ),
        out_specs=(P("block", "dp"), P("block", "dp", None)),
        check_vma=False,
    )
```

profile of v0, /device:TPU:0, one launch (start us, length us, event | category | flops | bytes accessed | tf_op | source)
XLA Modules:
  0.0 658.5 jit_solution(3671275075217711242)
XLA Ops:
  9.4 14.2 %gather_fusion.1 = f32[4096,3]{1,0:T(8,128)} fusion(f32[3,256]{0,1:T(8,128)S(1)} %copy.75, s32[4096]{0:T(1024)S(1)} %broadcast_clamp_fusion.1), kind=kCustom, calls=%fused_computation.1 | custom fusion | bytes 114688 | tf_op jit(solution)/shard_map/jvp(jvp())/gather | solution.py:50
  26.5 25.9 %gather_fusion.2 = s32[4096]{0:T(1024)S(1)} fusion(s32[256]{0:T(256)S(1)} %copy-done.1, s32[4096]{0:T(1024)S(1)} %broadcast_clamp_fusion.1), kind=kCustom, calls=%fused_computation.2 | custom fusion | bytes 49152 | tf_op jit(solution)/shard_map/gather | solution.py:40
  53.5 2.7 multiply_reduce_fusion.3
  61.7 4.2 copy.82
  70.5 4.3 copy.81
  82.0 446.8 %while.11 = (s32[]{:T(128)}, f32[16,64,256]{2,1,0:T(8,128)}, f32[16,16]{1,0:T(8,128)}, s32[16,256,1]{1,2,0:T(1,128)}, f32[3,16,256]{0,2,1:T(8,128)S(1)}, /*index...) while((s32[]{:T(128)}, f32[16,64,256]{2,1,0:T(8,128)}, ...), condition=%wide.region_6.7_spmd.clone, body=%wide.region_2.6_spmd.clone.sunk | while | flops 708266368 | bytes 27910064 | solution.py:81
  85.2 15.4 %gather_fusion = f32[4096,3]{1,0:T(8,128)} fusion(f32[3,256]{0,1:T(8,128)S(1)} %get-tuple-element.442, s32[4096]{0:T(1024)} %broadcast_clamp_fusion.3), kind=kCustom, calls=%fused_computation.clone.clone.1 | custom fusion | bytes 114688 | tf_op jit(solution)/shard_map/while/body/eval_jaxpr/transpose(jvp(transpose(jvp())))/gather | solution.py:50
  113.1 15.4 %gather_fusion = f32[4096,3]{1,0:T(8,128)} fusion(f32[3,256]{0,1:T(8,128)S(1)} %get-tuple-element.442, s32[4096]{0:T(1024)} %broadcast_clamp_fusion.3), kind=kCustom, calls=%fused_computation.clone.clone.1 | custom fusion | bytes 114688 | tf_op jit(solution)/shard_map/while/body/eval_jaxpr/transpose(jvp(transpose(jvp())))/gather | solution.py:50
  131.4 2.7 add_reduce_fusion.2
  141.0 15.4 %gather_fusion = f32[4096,3]{1,0:T(8,128)} fusion(f32[3,256]{0,1:T(8,128)S(1)} %get-tuple-element.442, s32[4096]{0:T(1024)} %broadcast_clamp_fusion.3), kind=kCustom, calls=%fused_computation.clone.clone.1 | custom fusion | bytes 114688 | tf_op jit(solution)/shard_map/while/body/eval_jaxpr/transpose(jvp(transpose(jvp())))/gather | solution.py:50
  168.9 15.4 %gather_fusion = f32[4096,3]{1,0:T(8,128)} fusion(f32[3,256]{0,1:T(8,128)S(1)} %get-tuple-element.442, s32[4096]{0:T(1024)} %broadcast_clamp_fusion.3), kind=kCustom, calls=%fused_computation.clone.clone.1 | custom fusion | bytes 114688 | tf_op jit(solution)/shard_map/while/body/eval_jaxpr/transpose(jvp(transpose(jvp())))/gather | solution.py:50
  196.8 15.4 %gather_fusion = f32[4096,3]{1,0:T(8,128)} fusion(f32[3,256]{0,1:T(8,128)S(1)} %get-tuple-element.442, s32[4096]{0:T(1024)} %broadcast_clamp_fusion.3), kind=kCustom, calls=%fused_computation.clone.clone.1 | custom fusion | bytes 114688 | tf_op jit(solution)/shard_map/while/body/eval_jaxpr/transpose(jvp(transpose(jvp())))/gather | solution.py:50
  224.8 15.4 %gather_fusion = f32[4096,3]{1,0:T(8,128)} fusion(f32[3,256]{0,1:T(8,128)S(1)} %get-tuple-element.442, s32[4096]{0:T(1024)} %broadcast_clamp_fusion.3), kind=kCustom, calls=%fused_computation.clone.clone.1 | custom fusion | bytes 114688 | tf_op jit(solution)/shard_map/while/body/eval_jaxpr/transpose(jvp(transpose(jvp())))/gather | solution.py:50
  252.7 15.4 %gather_fusion = f32[4096,3]{1,0:T(8,128)} fusion(f32[3,256]{0,1:T(8,128)S(1)} %get-tuple-element.442, s32[4096]{0:T(1024)} %broadcast_clamp_fusion.3), kind=kCustom, calls=%fused_computation.clone.clone.1 | custom fusion | bytes 114688 | tf_op jit(solution)/shard_map/while/body/eval_jaxpr/transpose(jvp(transpose(jvp())))/gather | solution.py:50
  280.6 15.4 %gather_fusion = f32[4096,3]{1,0:T(8,128)} fusion(f32[3,256]{0,1:T(8,128)S(1)} %get-tuple-element.442, s32[4096]{0:T(1024)} %broadcast_clamp_fusion.3), kind=kCustom, calls=%fused_computation.clone.clone.1 | custom fusion | bytes 114688 | tf_op jit(solution)/shard_map/while/body/eval_jaxpr/transpose(jvp(transpose(jvp())))/gather | solution.py:50
  308.5 15.4 %gather_fusion = f32[4096,3]{1,0:T(8,128)} fusion(f32[3,256]{0,1:T(8,128)S(1)} %get-tuple-element.442, s32[4096]{0:T(1024)} %broadcast_clamp_fusion.3), kind=kCustom, calls=%fused_computation.clone.clone.1 | custom fusion | bytes 114688 | tf_op jit(solution)/shard_map/while/body/eval_jaxpr/transpose(jvp(transpose(jvp())))/gather | solution.py:50
  336.5 15.4 %gather_fusion = f32[4096,3]{1,0:T(8,128)} fusion(f32[3,256]{0,1:T(8,128)S(1)} %get-tuple-element.442, s32[4096]{0:T(1024)} %broadcast_clamp_fusion.3), kind=kCustom, calls=%fused_computation.clone.clone.1 | custom fusion | bytes 114688 | tf_op jit(solution)/shard_map/while/body/eval_jaxpr/transpose(jvp(transpose(jvp())))/gather | solution.py:50
  364.4 15.4 %gather_fusion = f32[4096,3]{1,0:T(8,128)} fusion(f32[3,256]{0,1:T(8,128)S(1)} %get-tuple-element.442, s32[4096]{0:T(1024)} %broadcast_clamp_fusion.3), kind=kCustom, calls=%fused_computation.clone.clone.1 | custom fusion | bytes 114688 | tf_op jit(solution)/shard_map/while/body/eval_jaxpr/transpose(jvp(transpose(jvp())))/gather | solution.py:50
  392.3 15.4 %gather_fusion = f32[4096,3]{1,0:T(8,128)} fusion(f32[3,256]{0,1:T(8,128)S(1)} %get-tuple-element.442, s32[4096]{0:T(1024)} %broadcast_clamp_fusion.3), kind=kCustom, calls=%fused_computation.clone.clone.1 | custom fusion | bytes 114688 | tf_op jit(solution)/shard_map/while/body/eval_jaxpr/transpose(jvp(transpose(jvp())))/gather | solution.py:50
  420.3 15.4 %gather_fusion = f32[4096,3]{1,0:T(8,128)} fusion(f32[3,256]{0,1:T(8,128)S(1)} %get-tuple-element.442, s32[4096]{0:T(1024)} %broadcast_clamp_fusion.3), kind=kCustom, calls=%fused_computation.clone.clone.1 | custom fusion | bytes 114688 | tf_op jit(solution)/shard_map/while/body/eval_jaxpr/transpose(jvp(transpose(jvp())))/gather | solution.py:50
  448.2 15.4 %gather_fusion = f32[4096,3]{1,0:T(8,128)} fusion(f32[3,256]{0,1:T(8,128)S(1)} %get-tuple-element.442, s32[4096]{0:T(1024)} %broadcast_clamp_fusion.3), kind=kCustom, calls=%fused_computation.clone.clone.1 | custom fusion | bytes 114688 | tf_op jit(solution)/shard_map/while/body/eval_jaxpr/transpose(jvp(transpose(jvp())))/gather | solution.py:50
  476.1 15.4 %gather_fusion = f32[4096,3]{1,0:T(8,128)} fusion(f32[3,256]{0,1:T(8,128)S(1)} %get-tuple-element.442, s32[4096]{0:T(1024)} %broadcast_clamp_fusion.3), kind=kCustom, calls=%fused_computation.clone.clone.1 | custom fusion | bytes 114688 | tf_op jit(solution)/shard_map/while/body/eval_jaxpr/transpose(jvp(transpose(jvp())))/gather | solution.py:50
  504.0 15.4 %gather_fusion = f32[4096,3]{1,0:T(8,128)} fusion(f32[3,256]{0,1:T(8,128)S(1)} %get-tuple-element.442, s32[4096]{0:T(1024)} %broadcast_clamp_fusion.3), kind=kCustom, calls=%fused_computation.clone.clone.1 | custom fusion | bytes 114688 | tf_op jit(solution)/shard_map/while/body/eval_jaxpr/transpose(jvp(transpose(jvp())))/gather | solution.py:50
  531.3 22.7 %scatter_fusion = f32[3,256]{0,1:T(8,128)S(1)} fusion(f32[3,256]{0,1:T(8,128)S(1)} %neg.22, s32[4096]{0:T(1024)S(1)} %bitcast.177, f32[4096,3]{1,0:T(8,128)} %bitcast.170), kind=kCustom, calls=%fused_computation.5 | custom fusion | flops 12288 | bytes 163840 | tf_op jit(solution)/shard_map/jvp(transpose(jvp()))/scatter-add | solution.py:50
  555.4 8.9 %reduce-scatter.2.cloned.1.call-done = f32[16,8,256]{2,1,0:T(8,128)} async-done(((f32[16,64,256]{2,1,0:T(8,128)}), f32[16,8,256]{2,1,0:T(8,128)}) %reduce-scatter.2.cloned.1.call-update) | async-done | bytes 131088 | tf_op jit(solution)/shard_map/reduce_scatter | solution.py:133
  565.2 10.3 %all_gather.6 = f32[64,2048]{1,0:T(8,128)S(1)} all-gather(f32[16,2048]{1,0:T(8,128)S(1)} %bitcast.175), channel_id=1, replica_groups=mesh['dp'=4,'block'=8] {'dp'}, dimensions={0}, use_global_device_ids=true | all-gather | bytes 655360 | tf_op jit(solution)/shard_map/all_gather | solution.py:134
  575.5 6.3 fusion.25
  582.1 37.4 %all-reduce = (f32[64,64]{0,1:T(8,128)S(1)}, f32[64]{0:T(128)S(1)}) all-reduce(f32[64,64]{0,1:T(8,128)S(1)} %fusion.35, f32[64]{0:T(128)S(1)} %multiply_dynamic-update-slice_fusion), channel_id=1, replica_groups=mesh['dp'=4,'block'=8] {'dp','block'}, use_global_device_ids=true, to_apply=%region_8.9 | all-reduce | flops 4160 | bytes 33280 | tf_op jit(solution)/shard_map/psum | solution.py:141
  619.8 5.8 cholesky.17
  627.0 4.9 custom-call.10
  632.6 11.5 %all_gather.7 = f32[2048,64]{0,1:T(8,128)S(1)} all-gather(f32[512,64]{0,1:T(8,128)S(1)} %fusion.63), channel_id=1, replica_groups=mesh['dp'=4,'block'=8] {'dp'}, dimensions={0}, use_global_device_ids=true | all-gather | bytes 655360 | tf_op jit(solution)/shard_map/all_gather | solution.py:146
  644.1 6.8 %fusion.28 = f32[1,512,2048]{2,1,0:T(8,128)} fusion(f32[1,512,2048]{2,1,0:T(8,128)} %param.33, f32[64,512]{1,0:T(8,128)S(1)} %fusion.25, f32[2048,64]{0,1:T(8,128)S(1)} %all_gather.7), kind=kOutput, calls=%fused_computation.45 | convolution fusion | flops 807403520 | bytes 9043968 | tf_op jit(solution)/shard_map/dot_general | solution.py:147
  (608 shorter events, 227.0 us)
Async XLA Ops:
  7.2 49.9 %copy-start = (f32[4,256]{1,0:T(4,128)S(1)}, f32[4,256]{1,0:T(4,128)}, u32[]{:S(2)}) copy-start(f32[4,256]{1,0:T(4,128)} %param.32) | copy-start | bytes 12292
  7.2 557.1 %reduce-scatter.2.cloned.1.call-start = ((), (), s32[]{:S(2)}) async-start(), calls=%async_computation.1 | async-start | bytes 1179648 | tf_op jit(solution)/shard_map/reduce_scatter | solution.py:133
  26.5 27.0 %copy-start.13 = (f32[16,256]{1,0:T(8,128)}, f32[16,256]{1,0:T(8,128)S(1)}, u32[]{:S(2)}) copy-start(f32[16,256]{1,0:T(8,128)S(1)} %get-tuple-element.297) | copy-start | bytes 49156
  26.5 25.9 %copy-start.26 = (f32[4,128]{1,0:T(4,128)S(1)}, f32[4,128]{1,0:T(4,128)}, u32[]{:S(2)}) copy-start(f32[4,128]{1,0:T(4,128)} %param.26) | copy-start | bytes 6148
  56.7 9.2 %copy-start.7 = (f32[256,256]{1,0:T(8,128)}, f32[256,256]{1,0:T(8,128)S(1)}, u32[]{:S(2)}) copy-start(f32[256,256]{1,0:T(8,128)S(1)} %get-tuple-element.312) | copy-start | bytes 786436
  61.7 4.8 copy-start.10
  70.3 4.4 copy-start.14
  70.4 4.3 copy-start.5
  70.4 4.3 copy-start.6
  76.0 6.0 copy-start.22
  106.1 3.8 copy-start.23
  134.0 3.8 copy-start.23
  162.0 3.8 copy-start.23
  189.9 3.8 copy-start.23
  217.8 3.8 copy-start.23
  245.7 3.8 copy-start.23
  273.7 3.8 copy-start.23
  301.6 3.8 copy-start.23
  329.5 3.8 copy-start.23
  357.4 3.8 copy-start.23
  385.4 3.8 copy-start.23
  413.3 3.8 copy-start.23
  441.2 3.8 copy-start.23
  469.1 3.8 copy-start.23
  497.1 3.8 copy-start.23
  525.0 3.8 copy-start.23
  528.8 25.5 %copy-start.25 = (f32[256]{0:T(256)S(1)}, f32[256]{0:T(256)}, u32[]{:S(2)}) copy-start(f32[256]{0:T(256)} %get-tuple-element.302) | copy-start | bytes 3076
  528.8 25.7 %slice-start = ((f32[256,256]{1,0:T(8,128)}), f32[64,256]{1,0:T(8,128)S(1)}, s32[]{:S(2)}) async-start(f32[256,256]{1,0:T(8,128)} %param.30), calls=%async_computation.2 | async-start | bytes 131072 | tf_op jit(solution)/shard_map/slice | solution.py:108
  528.9 25.7 %copy-start.32 = (s32[16]{0:T(128)S(1)}, s32[16]{0:T(128)}, u32[]{:S(2)}) copy-start(s32[16]{0:T(128)} %constant.169) | copy-start | bytes 196
  528.9 26.3 %copy-start.24 = (s32[8]{0:T(128)S(1)}, s32[8]{0:T(128)}, u32[]{:S(2)}) copy-start(s32[8]{0:T(128)} %get-tuple-element.541) | copy-start | bytes 100
  575.5 44.1 %copy-start.30 = (f32[64]{0:T(128)S(1)}, f32[64]{0:T(128)}, u32[]{:S(2)}) copy-start(f32[64]{0:T(128)} %param.25) | copy-start | bytes 772
  644.1 6.8 %copy-start.31 = (f32[64]{0:T(128)S(1)}, f32[64]{0:T(128)}, u32[]{:S(2)}) copy-start(f32[64]{0:T(128)} %param.24) | copy-start | bytes 772
  (93 other events, 238.1 us)
Sparse Core Ops, SparseCore 0:
  528.9 35.2 reduce-scatter.1
where the time goes:
time: 666 us; the launch traced here: 658 us
  local copies, waits for them, and re-layouts  318 us (48%)
  other arithmetic  185 us (28%)
  matrix products  70.8 us (11%)
  blocking collectives  59.2 us (9%)
  between operations  14.6 us (2%)
  waiting for transfers between devices  8.89 us (1%)
    gather x17, local copies, waits for them, and re-layouts, site_energy(): displace = coords[:, neighbour_at] - coords[:, None, :]  261 us
    reduce_sum x16, other arithmetic, site_energy(): descriptor = jnp.sum(radial[None] * embedded, axis=1) / slot_count  42.8 us
    dot_general x50, matrix products, site_energy(): jnp.dot(middle.T, first_layer, precision=highest) + middle_bias[:, None]  42.1 us
    reduce_sum x17, other arithmetic, site_energy(): distance_sq = jnp.sum(displace * displace, axis=0)  40.8 us
    psum x1, blocking collectives, local(): gram_sum = lax.psum(partial_value, ('dp', 'block'))  37.4 us
    gather x2, local copies, waits for them, and re-layouts, observations(): near_species = atom_species[neighbour_at]  25.9 us
    scatter-add x1, other arithmetic, site_energy(): displace = coords[:, neighbour_at] - coords[:, None, :]  22.7 us
    gather x17, other arithmetic, site_energy(): displace = coords[:, neighbour_at] - coords[:, None, :]  21.1 us
  transfers between devices with their start and end apart: 1, of which 1 were waited for; matrix products, arithmetic and copies ran while one was open for 4% of the time, Pallas kernels for 0%

commit v1 on v0

v1 whole, which is shorter than its diff:
```python
import functools

import jax
import jax.numpy as jnp
from jax import lax
from jax.experimental import pallas as pl
from jax.experimental.pallas import tpu as pltpu
from jax.sharding import PartitionSpec as P

OBS = 64
AUX = 128

radial_width = 4.0
forgetting = 0.98
highest = lax.Precision.HIGHEST


def contract(left, right, left_dim, right_dim):
    return lax.dot_general(
        left,
        right,
        (((left_dim,), (right_dim,)), ((), ())),
        precision=highest,
        preferred_element_type=jnp.float32,
    )


def observe_kernel(
    weighting,
    tagged_ref,
    observed_ref,
    positions_ref,
    neighbours_ref,
    species_ref,
    scale_ref,
    shift_ref,
    first_weight_ref,
    first_bias_ref,
    middle_ref,
    middle_bias_ref,
    energy_ref,
    out_ref,
    radial_ref,
    slope_ref,
    near_ref,
    scale_cols,
    shift_cols,
    desc_ref,
):
    atoms = positions_ref.shape[1]
    structs = tagged_ref.shape[1]
    struct_size = atoms // structs
    slots = neighbours_ref.shape[0]
    species_count, channels = scale_ref.shape
    hidden = middle_ref.shape[1]
    blocks = out_ref.shape[0]
    order = out_ref.shape[2] - AUX
    block_rows = order // hidden
    rows = blocks * block_rows

    lane = lax.broadcasted_iota(jnp.int32, (1, atoms), 1)
    start = jnp.zeros_like(lane)
    tag = jnp.zeros_like(lane)
    comp = jnp.zeros_like(lane)
    for s in range(structs):
        here = jnp.logical_and(lane >= s * struct_size, lane < (s + 1) * struct_size)
        start = jnp.where(here, s * struct_size, start)
        tag = jnp.where(here, tagged_ref[0, s], tag)
        comp = jnp.where(here, observed_ref[0, s] & 3, comp)
    inside = lane - start
    own = species_ref[...]

    for base in range(0, atoms, 128):
        cols = slice(base, base + 128)
        listed = neighbours_ref[:, cols]
        near = jnp.minimum(listed, struct_size - 1)
        index = near + (start[:, cols] - base)

        def pick(row):
            wide = jnp.broadcast_to(row, (slots, 128))
            return jnp.take_along_axis(wide, index, axis=1, mode="promise_in_bounds")

        shift_by = []
        for axis in range(3):
            mine = positions_ref[axis : axis + 1, cols]
            shift_by.append(pick(mine) - mine)
        distance_sq = shift_by[0] * shift_by[0]
        for axis in range(1, 3):
            distance_sq = distance_sq + shift_by[axis] * shift_by[axis]
        live = listed < struct_size
        radial = jnp.where(live, jnp.exp(-distance_sq / radial_width), 0.0)
        near_species = pick(own[:, cols].astype(jnp.float32))
        kind = comp[:, cols]
        along = jnp.where(kind == 1, shift_by[0], 0.0)
        along = jnp.where(kind == 2, shift_by[1], along)
        along = jnp.where(kind == 3, shift_by[2], along)
        moved = (near == tag[:, cols]).astype(jnp.float32) - (
            inside[:, cols] == tag[:, cols]
        ).astype(jnp.float32)
        slope = (-2.0 / radial_width) * radial * along * moved
        for k in range(slots):
            radial_ref[k, :, cols] = jnp.broadcast_to(radial[k : k + 1], (8, 128))
            slope_ref[k, :, cols] = jnp.broadcast_to(slope[k : k + 1], (8, 128))
            near_ref[k, :, cols] = jnp.broadcast_to(near_species[k : k + 1], (8, 128))

    scale_t = scale_ref[...].T
    shift_t = shift_ref[...].T
    for i in range(species_count):
        scale_cols[i] = jnp.broadcast_to(scale_t[:, i : i + 1], (channels, 128))
        shift_cols[i] = jnp.broadcast_to(shift_t[:, i : i + 1], (channels, 128))

    def embed(group, _):
        group_rows = pl.ds(pl.multiple_of(group * 8, 8), 8)
        scales = [scale_cols[i, group_rows, :] for i in range(species_count)]
        shifts = [shift_cols[i, group_rows, :] for i in range(species_count)]
        for base in range(0, atoms, 128):
            cols = slice(base, base + 128)
            total = jnp.zeros((8, 128), jnp.float32)
            moved = jnp.zeros((8, 128), jnp.float32)
            for k in range(slots):
                radial = radial_ref[k, :, cols]
                slope = slope_ref[k, :, cols]
                near = near_ref[k, :, cols]
                scale, shift = scales[-1], shifts[-1]
                for i in range(species_count - 1):
                    same = near == float(i)
                    scale = jnp.where(same, scales[i], scale)
                    shift = jnp.where(same, shifts[i], shift)
                scaled = radial * scale
                bent = jnp.tanh(scaled + shift)
                total = total + radial * bent
                moved = moved + slope * (bent + scaled * (1.0 - bent * bent))
            desc_ref[group_rows, cols] = total * (1.0 / slots)
            desc_ref[group_rows, slice(atoms + base, atoms + base + 128)] = moved * (
                1.0 / slots
            )
        return 0

    lax.fori_loop(0, channels // 8, embed, 0)

    first_bias = jnp.broadcast_to(first_bias_ref[...], (8, hidden)).T[:, :1]
    middle_bias = jnp.broadcast_to(middle_bias_ref[...], (8, hidden)).T[:, :1]
    energy_t = energy_ref[...].T
    lower = contract(first_weight_ref[...], desc_ref[...], 0, 0)
    first = jnp.tanh(lower[:, :atoms] + first_bias)
    first_moved = (1.0 - first * first) * lower[:, atoms:]
    upper = contract(middle_ref[...], jnp.concatenate([first, first_moved], axis=1), 0, 0)
    second = jnp.tanh(upper[:, :atoms] + middle_bias)
    moved = upper[:, atoms:]
    readout = jnp.broadcast_to(
        energy_t[:, species_count - 1 : species_count], (hidden, atoms)
    )
    for i in range(species_count - 1):
        readout = jnp.where(own == i, energy_t[:, i : i + 1], readout)
    gate = readout * (1.0 - second * second)
    mean = jnp.where(comp == 0, 1.0 / struct_size, 0.0)
    value = mean * jnp.sum(readout * second, axis=0, keepdims=True) - jnp.sum(
        gate * moved, axis=0, keepdims=True
    )
    bend = 2.0 * second * gate * moved + mean * gate

    struct_row = lax.broadcasted_iota(jnp.int32, (structs, atoms), 0)
    member = jnp.where(start == struct_row * struct_size, weighting, 0.0)
    struct_value = jnp.sum(member * value, axis=1, keepdims=True)
    left = jnp.concatenate([-first_moved[:rows], first[:rows]], axis=1)
    right = jnp.concatenate([gate, bend], axis=1)
    member_twice = jnp.concatenate([member, member], axis=1)
    spread = (left[:, None, :] * member_twice[None]).reshape(rows * structs, 2 * atoms)
    terms = contract(spread, right, 1, 1)
    for h in range(rows):
        place = (h % block_rows) * hidden
        out_ref[h // block_rows, :, place : place + hidden] = terms[
            h * structs : (h + 1) * structs
        ]
    row = lax.broadcasted_iota(jnp.int32, (structs, AUX), 0)
    column = lax.broadcasted_iota(jnp.int32, (structs, AUX), 1)
    observed = jnp.zeros((structs, AUX), jnp.int32)
    for s in range(structs):
        observed = jnp.where(row == s, observed_ref[0, s], observed)
    aux = jnp.where(
        column < OBS, (observed == column).astype(jnp.float32), struct_value
    )
    for b in range(blocks):
        out_ref[b, :, order:] = aux


def observe(
    blocks,
    order,
    weighting,
    positions,
    neighbours,
    atom_species,
    tagged_atom,
    observed_in,
    embed_scale,
    embed_shift,
    first_weight,
    first_bias,
    middle_weight,
    middle_bias,
    energy_weight,
):
    atoms = positions.shape[1]
    structs = tagged_atom.shape[0]
    slots = neighbours.shape[0]
    species_count, channels = embed_scale.shape
    vmem = pl.BlockSpec(memory_space=pltpu.VMEM)
    smem = pl.BlockSpec(memory_space=pltpu.SMEM)
    return pl.pallas_call(
        functools.partial(observe_kernel, weighting),
        out_shape=jax.ShapeDtypeStruct((blocks, structs, order + AUX), jnp.float32),
        in_specs=[smem, smem] + [vmem] * 10,
        out_specs=vmem,
        scratch_shapes=[
            pltpu.VMEM((slots, 8, atoms), jnp.float32),
            pltpu.VMEM((slots, 8, atoms), jnp.float32),
            pltpu.VMEM((slots, 8, atoms), jnp.float32),
            pltpu.VMEM((species_count, channels, 128), jnp.float32),
            pltpu.VMEM((species_count, channels, 128), jnp.float32),
            pltpu.VMEM((channels, 2 * atoms), jnp.float32),
        ],
    )(
        tagged_atom[None],
        observed_in[None],
        positions,
        neighbours,
        atom_species[None],
        embed_scale,
        embed_shift,
        first_weight,
        first_bias[None],
        middle_weight,
        middle_bias[None],
        energy_weight,
    )


def local(
    positions,
    neighbours,
    atom_species,
    tagged_atom,
    observed_in,
    targets,
    noise_level,
    embed_scale,
    embed_shift,
    first_weight,
    first_bias,
    middle_weight,
    middle_bias,
    energy_weight,
    covariance,
):
    group_count = lax.axis_size("dp")
    block_count = lax.axis_size("block")
    block_order = covariance.shape[2]
    row_share = covariance.shape[1]
    hidden = middle_weight.shape[1]
    block_rows = block_order // hidden
    window = middle_weight[: block_rows * block_count]
    obs_group = OBS // group_count
    weighting = OBS / (tagged_atom.shape[0] * group_count * block_count)
    terms = observe(
        block_count,
        block_order,
        weighting,
        positions,
        neighbours,
        atom_species,
        tagged_atom,
        observed_in,
        embed_scale,
        embed_shift,
        first_weight,
        first_bias,
        middle_weight,
        middle_bias,
        energy_weight,
    )
    chosen = (
        observed_in[:, None] == jnp.arange(obs_group, dtype=jnp.int32)[None, :]
    ).astype(jnp.float32)
    by_obs = jnp.einsum("sq,bsn->bqn", chosen, terms, precision=highest)
    mine = lax.psum_scatter(by_obs, "block", scatter_dimension=0, tiled=True)[0]
    everyone = lax.all_gather(mine, "dp", axis=0, tiled=True)
    jacobian = everyone[:, :block_order]
    predicted = everyone[:, -1]
    cov_rows = covariance[0]
    product = jnp.dot(cov_rows, jacobian.T, precision=highest)
    columns = lax.dynamic_slice_in_dim(jacobian, lax.axis_index("dp") * row_share, row_share, 1)
    partial_value = jnp.dot(columns, product, precision=highest)
    gram_sum = lax.psum(partial_value, ("dp", "block"))
    gram_sum = 0.5 * (gram_sum + gram_sum.T) + jnp.diag(noise_level)
    factor = jnp.linalg.cholesky(gram_sum)
    inverse = jax.scipy.linalg.cho_solve((factor, True), jnp.eye(OBS, dtype=jnp.float32))
    gain_rows = jnp.dot(product, inverse, precision=highest)
    product_all = lax.all_gather(product, "dp", axis=0, tiled=True)
    update = jnp.dot(gain_rows, product_all.T, precision=highest)
    innovation = targets - predicted
    block_window = lax.dynamic_slice_in_dim(
        window.reshape(block_count, block_order), lax.axis_index("block"), 1, 0
    )
    window_rows = lax.dynamic_slice_in_dim(
        block_window, lax.axis_index("dp") * row_share, row_share, 1
    )
    new_weights = window_rows + jnp.dot(gain_rows, innovation, precision=highest)[None, :]
    new_covariance = ((cov_rows - update) / forgetting)[None]
    return (new_weights, new_covariance)


def solution(mesh):
    return jax.shard_map(
        local,
        mesh=mesh,
        in_specs=(
            P(None, ("dp", "block")),
            P(None, ("dp", "block")),
            P(("dp", "block")),
            P(("dp", "block")),
            P(("dp", "block")),
            P(),
            P(),
            P(),
            P(),
            P(),
            P(),
            P(),
            P(),
            P(),
            P("block", "dp", None),
        ),
        out_specs=(P("block", "dp"), P("block", "dp", None)),
        check_vma=False,
    )
```

time: 666 us -> 145 us (0.22); the launches traced: 658 us -> 145 us
  local copies, waits for them, and re-layouts: 318 us -> 1.24 us
  other arithmetic: 185 us -> 12.2 us
  matrix products: 70.8 us -> 17.6 us
  waiting for transfers between devices: 8.89 us -> 34.8 us
    gather x20 -> x0, local copies, waits for them, and re-layouts: 287 us -> none  [the longest x17 261 us: site_energy(): displace = coords[:, neighbour_at] - coords[:, None, :]]
    reduce_sum x38 -> x0, other arithmetic: 87.6 us -> none  [the longest x16 42.8 us: site_energy(): descriptor = jnp.sum(radial[None] * embedded, axis=1) / slot_count]
    dot_general x72 -> x2, matrix products: 62.7 us -> 9.54 us  [the longest x1 6.78 us: local(): update = jnp.dot(gain_rows, product_all.T, precision=highest)]
    scatter-add x17 -> x0, other arithmetic: 35.6 us -> none  [the longest x1 22.7 us: site_energy(): displace = coords[:, neighbour_at] - coords[:, None, :]]
    reduce_scatter x1, waiting for transfers between devices: 8.87 us -> 34.8 us  [local(): mine = lax.psum_scatter(by_obs, 'block', scatter_dimension=0, tiled=True)[0]]
    gather x18 -> x0, other arithmetic: 21.1 us -> none  [the longest x17 21.1 us: site_energy(): displace = coords[:, neighbour_at] - coords[:, None, :]]
    unnamed x64 -> x4, local copies, waits for them, and re-layouts: 17.8 us -> 0.01 us
    mul x34 -> x0, other arithmetic: 11 us -> none  [the longest x16 10.9 us: predict(): return jnp.sum(chosen * value_rows, axis=1) * weighting]
  transfers between devices with their start and end apart: 1 -> 1, of which waited for: 1 -> 1; matrix products, arithmetic and copies ran while one was open for 4% -> 1% of each run, Pallas kernels for 0% -> 0%
where the time goes in v1:
time: 145 us
  blocking collectives  58.8 us (41%)
  waiting for transfers between devices  34.8 us (24%)
  matrix products  17.6 us (12%)
  between operations  14.1 us (10%)
  other arithmetic  12.2 us (8%)
  Pallas kernels  6.09 us (4%)
    psum x1, blocking collectives, local(): gram_sum = lax.psum(partial_value, ('dp', 'block'))  37 us
    reduce_scatter x1, waiting for transfers between devices, local(): mine = lax.psum_scatter(by_obs, 'block', scatter_dimension=0, tiled=True)[0]  34.8 us
    all_gather x1, blocking collectives, local(): product_all = lax.all_gather(product, 'dp', axis=0, tiled=True)  11.5 us
    all_gather x1, blocking collectives, local(): everyone = lax.all_gather(mine, 'dp', axis=0, tiled=True)  10.3 us
    dot_general x1, matrix products, local(): update = jnp.dot(gain_rows, product_all.T, precision=highest)  6.78 us
    another operation x3, other arithmetic, local(): factor = jnp.linalg.cholesky(gram_sum)  6.52 us
    dot_general x1, matrix products, local(): product = jnp.dot(cov_rows, jacobian.T, precision=highest)  6.28 us
    pallas_call x1, Pallas kernels, observe(): pl.pallas_call(functools.partial(observe_kernel, weighting), out_shape=ja...  6.09 us
  transfers between devices with their start and end apart: 1, of which 1 were waited for; matrix products, arithmetic and copies ran while one was open for 1% of the time, Pallas kernels for 0%

profile of v1, /device:TPU:0, one launch (start us, length us, event | category | flops | bytes accessed | tf_op | source)
XLA Modules:
  0.0 144.9 jit_solution(15112236801556605903)
XLA Ops:
  7.2 0.0 reduce-scatter.2.cloned.1.call-start
  7.2 6.1 %shard_map.158 = f32[8,8,2176]{2,1,0:T(8,128)} custom-call(s32[1,8]{1,0:T(1,128)} %bitcast.59, s32[1,8]{1,0:T(1,128)} %bitcast.55, f32[3,256]{1,0:T(4,128)} %positions_ref.1, s32[16,256]{1,0:T(8,128)} %neighbours_ref.1, s32[1,256]{1,0:T(1,128)} %bitcast.56, f32[4,128]{1,0:T(4,128)} %scale_ref.1, f32[4,128]{1,0:T(4,128)} %shift_ref.1, ...), custom_call_target="tpu_custom_call" | custom-call | tf_op jit(solution)/shard_map/pallas_call | solution.py:210
  13.3 2.8 %convolution_bitcast_fusion = f32[8,16,2176]{2,1,0:T(8,128)} fusion(f32[8,8,2176]{2,1,0:T(8,128)} %shard_map.158, s32[8]{0:T(128)} %param.19), kind=kOutput, calls=%fused_computation.5 | convolution fusion | flops 26738816 | bytes 1671200 | tf_op jit(solution)/shard_map/sq,bsn->bqn/dot_general | solution.py:285
  16.1 0.0 copy-start
  16.1 0.0 reduce-scatter.2.cloned.1.call-update
  16.1 0.8 slice.27
  17.0 34.8 %reduce-scatter.2.cloned.1.call-done = f32[1,16,2176]{2,1,0:T(8,128)} async-done(((f32[8,16,2176]{2,1,0:T(8,128)}), f32[1,16,2176]{2,1,0:T(8,128)}) %reduce-scatter.2.cloned.1.call-update) | async-done | bytes 139280 | tf_op jit(solution)/shard_map/reduce_scatter | solution.py:286
  51.8 10.3 %all-gather = f32[1,64,2176]{2,1,0:T(8,128)S(1)} all-gather(f32[1,16,2176]{2,1,0:T(8,128)} %reduce-scatter.2.cloned.1.call-done), channel_id=2, replica_groups=mesh['dp'=4,'block'=8] {'dp'}, dimensions={1}, use_global_device_ids=true | all-gather | bytes 696320 | tf_op jit(solution)/shard_map/all_gather | solution.py:287
  62.1 0.2 slice_reduce_fusion
  62.4 6.3 %fusion = f32[64,512]{1,0:T(8,128)S(1)} fusion(f32[1,512,2048]{2,1,0:T(8,128)} %param.29, f32[64,2176]{1,0:T(8,128)S(1)} %bitcast.53), kind=kOutput, calls=%fused_computation.1 | convolution fusion | flops 805306368 | bytes 4849664 | tf_op jit(solution)/shard_map/dot_general | solution.py:291
  68.6 0.3 fusion.4
  68.9 37.0 %psum.7 = f32[64,64]{0,1:T(8,128)S(1)} all-reduce(f32[64,64]{0,1:T(8,128)S(1)} %fusion.4), channel_id=1, replica_groups=mesh['dp'=4,'block'=8] {'dp','block'}, use_global_device_ids=true, to_apply=%region_1.0 | all-reduce | flops 4096 | bytes 32768 | tf_op jit(solution)/shard_map/psum | solution.py:294
  105.9 0.1 copy.21
  106.0 0.0 copy-done
  106.0 0.1 fusion.13
  106.1 0.1 copy.22
  106.2 5.8 %cholesky.17 = f32[64,64]{1,0:T(8,128)S(1)} custom-call(f32[64,64]{1,0:T(8,128)S(1)} %fusion.11), custom_call_target="Cholesky" | custom-call | tf_op jit(solution)/shard_map/jit(cholesky)/cholesky | solution.py:296
  112.1 0.6 compare_reduce_fusion
  112.7 0.7 fusion.6
  113.4 4.9 %custom-call.10 = f32[1,64,64]{1,2,0:T(8,128)S(1)} custom-call(f32[1,64,64]{2,1,0:T(8,128)S(1)} %fusion.6), custom_call_target="InvertDiagBlocksLowerTriangular" | custom-call | tf_op jit(solution)/shard_map/jit(_cho_solve)/triangular_solve | solution.py:297
  118.3 0.2 fusion.9
  118.5 0.2 fusion.7
  118.7 0.3 fusion.21
  119.0 11.5 %all_gather.7 = f32[2048,64]{0,1:T(8,128)S(1)} all-gather(f32[512,64]{0,1:T(8,128)S(1)} %bitcast.54), channel_id=1, replica_groups=mesh['dp'=4,'block'=8] {'dp'}, dimensions={0}, use_global_device_ids=true | all-gather | bytes 655360 | tf_op jit(solution)/shard_map/all_gather | solution.py:299
  130.5 0.0 copy-start.1
  130.5 6.8 %fusion.3 = f32[1,512,2048]{2,1,0:T(8,128)} fusion(f32[1,512,2048]{2,1,0:T(8,128)} %param.29, f32[512,64]{0,1:T(8,128)S(1)} %fusion.21, f32[2048,64]{0,1:T(8,128)S(1)} %all_gather.7), kind=kOutput, calls=%fused_computation.4 | convolution fusion | flops 807403520 | bytes 9043968 | tf_op jit(solution)/shard_map/dot_general | solution.py:300
  137.3 0.0 copy-done.1
  137.3 0.8 convolution_add_fusion
  (4 shorter events, 0.1 us)
Async XLA Ops:
  7.2 44.6 %reduce-scatter.2.cloned.1.call-start = ((), (), s32[]{:S(2)}) async-start(), calls=%async_computation.1 | async-start | bytes 1253376 | tf_op jit(solution)/shard_map/reduce_scatter | solution.py:286
  16.1 89.9 %copy-start = (f32[64]{0:T(128)S(1)}, f32[64]{0:T(128)}, u32[]{:S(2)}) copy-start(f32[64]{0:T(128)} %param.21) | copy-start | bytes 772
  130.5 6.8 %copy-start.1 = (f32[64]{0:T(128)S(1)}, f32[64]{0:T(128)}, u32[]{:S(2)}) copy-start(f32[64]{0:T(128)} %param.20) | copy-start | bytes 772
Sparse Core Ops, SparseCore 0:
  16.2 35.5 reduce-scatter.1

commit v2 on v1

--- a/solution.py
+++ b/solution.py
@@ -168,7 +168,7 @@
     spread = (left[:, None, :] * member_twice[None]).reshape(rows * structs, 2 * atoms)
     terms = contract(spread, right, 1, 1)
     for h in range(rows):
-        place = (h % block_rows) * hidden
+        place = AUX + (h % block_rows) * hidden
         out_ref[h // block_rows, :, place : place + hidden] = terms[
             h * structs : (h + 1) * structs
         ]
@@ -181,7 +181,7 @@
         column < OBS, (observed == column).astype(jnp.float32), struct_value
     )
     for b in range(blocks):
-        out_ref[b, :, order:] = aux
+        out_ref[b, :, :AUX] = aux
 
 
 def observe(
@@ -236,6 +236,307 @@
     )
 
 
+MESH = pl.DeviceIdType.MESH
+
+
+def exchange_kernel(
+    group_count,
+    block_count,
+    terms_ref,
+    cov_ref,
+    product_ref,
+    gram_ref,
+    aux_ref,
+    got,
+    jac,
+    cov_rows,
+    total,
+    gram_mine,
+    gram_near,
+    gram_sum,
+    gram_far,
+    cov_sem,
+    own_sem,
+    term_send,
+    term_recv,
+    jac_send,
+    jac_recv,
+    gram_send,
+    gram_recv,
+    far_send,
+    far_recv,
+    product_send,
+    product_recv,
+):
+    group = lax.axis_index("dp")
+    block = lax.axis_index("block")
+    structs, width = terms_ref.shape[1:]
+    obs_group = jac.shape[1]
+    row_share = cov_ref.shape[0]
+    half = (width - AUX) // 2
+    chunks = ((0, AUX + half), (AUX + half, half))
+    group_peers = [(o, lax.rem(group + o, group_count)) for o in range(1, group_count)]
+    block_peers = [(o, lax.rem(block + o, block_count)) for o in range(1, block_count)]
+
+    cov_copy = pltpu.make_async_copy(cov_ref, cov_rows, cov_sem)
+    cov_copy.start()
+    own_copy = pltpu.make_async_copy(terms_ref.at[block], got.at[0], own_sem)
+    own_copy.start()
+
+    barrier = pltpu.get_barrier_semaphore()
+    for _, peer in group_peers:
+        pl.semaphore_signal(
+            barrier, inc=1, device_id={"dp": peer}, device_id_type=MESH
+        )
+    for _, peer in block_peers:
+        pl.semaphore_signal(
+            barrier, inc=1, device_id={"block": peer}, device_id_type=MESH
+        )
+    pl.semaphore_wait(barrier, group_count + block_count - 2)
+
+    def send(source, target, send_sem, recv_sem, device_id):
+        copy = pltpu.make_async_remote_copy(
+            src_ref=source,
+            dst_ref=target,
+            send_sem=send_sem,
+            recv_sem=recv_sem,
+            device_id=device_id,
+            device_id_type=MESH,
+        )
+        copy.start()
+        return copy
+
+    term_copies = []
+    for c, (base, size) in enumerate(chunks):
+        cols = pl.ds(base, size)
+        term_copies.append(
+            [
+                send(
+                    terms_ref.at[peer, :, cols],
+                    got.at[o, :, cols],
+                    term_send.at[c, o - 1],
+                    term_recv.at[c, o - 1],
+                    {"block": peer},
+                )
+                for o, peer in block_peers
+            ]
+        )
+    own_copy.wait()
+
+    jac_copies = []
+    for c, (base, size) in enumerate(chunks):
+        cols = pl.ds(base, size)
+        for copy in term_copies[c]:
+            copy.wait_recv()
+        chosen = got[:, :, :AUX].reshape(block_count * structs, AUX).T[:obs_group]
+        pieces = got[:, :, cols].reshape(block_count * structs, size)
+        jac[group, :, cols] = contract(chosen, pieces, 1, 0)
+        jac_copies.append(
+            [
+                send(
+                    jac.at[group, :, cols],
+                    jac.at[group, :, cols],
+                    jac_send.at[c, o - 1],
+                    jac_recv.at[c, o - 1],
+                    {"dp": peer},
+                )
+                for o, peer in group_peers
+            ]
+        )
+
+    cov_copy.wait()
+    for c in range(2):
+        for copy in jac_copies[c]:
+            copy.wait_recv()
+        rows = jac[:, :, AUX + c * half : AUX + (c + 1) * half].reshape(OBS, half)
+        rows = jnp.concatenate([rows, jnp.zeros_like(rows)], axis=0)
+        part = contract(cov_rows[:, c * half : (c + 1) * half], rows, 1, 1)
+        if c == 0:
+            total[...] = part
+        else:
+            product = (total[...] + part).T
+    product_ref[group] = product[:OBS]
+    mine = jac[:, :, pl.ds(pl.multiple_of(AUX + group * row_share, 128), row_share)]
+    gram = contract(mine.reshape(OBS, row_share), product, 1, 1)
+    fold = OBS // 2
+    gram_mine[...] = gram[:fold] + pltpu.roll(gram[fold:], 64, 1)
+    gram_copies = [
+        send(
+            gram_mine,
+            gram_near.at[o - 1],
+            gram_send.at[o - 1],
+            gram_recv.at[o - 1],
+            {"dp": peer},
+        )
+        for o, peer in group_peers
+    ]
+    product_copies = [
+        send(
+            product_ref.at[group],
+            product_ref.at[group],
+            product_send.at[o - 1],
+            product_recv.at[o - 1],
+            {"dp": peer},
+        )
+        for o, peer in group_peers
+    ]
+    aux_ref[...] = jac[:, :, :AUX]
+    summed = gram_mine[...]
+    for i, copy in enumerate(gram_copies):
+        copy.wait_recv()
+        summed = summed + gram_near[i]
+    gram_sum[...] = summed
+    far_copies = [
+        send(
+            gram_sum,
+            gram_far.at[o - 1],
+            far_send.at[o - 1],
+            far_recv.at[o - 1],
+            {"block": peer},
+        )
+        for o, peer in block_peers
+    ]
+    for i, copy in enumerate(far_copies):
+        copy.wait_recv()
+        summed = summed + gram_far[i]
+    gram_ref[:fold] = summed
+    gram_ref[fold:] = pltpu.roll(summed, 64, 1)
+    for copy in product_copies:
+        copy.wait_recv()
+    for copies in term_copies + jac_copies + [gram_copies, far_copies, product_copies]:
+        for copy in copies:
+            copy.wait_send()
+
+
+def exchange(group_count, obs_group, terms, cov_rows):
+    block_count, structs, width = terms.shape
+    row_share, order = cov_rows.shape
+    vmem = pl.BlockSpec(memory_space=pltpu.VMEM)
+    fold = OBS // 2
+    dma = pltpu.SemaphoreType.DMA
+    near, far = group_count - 1, block_count - 1
+    return pl.pallas_call(
+        functools.partial(exchange_kernel, group_count, block_count),
+        out_shape=(
+            jax.ShapeDtypeStruct((group_count, OBS, row_share), jnp.float32),
+            jax.ShapeDtypeStruct((OBS, 128), jnp.float32),
+            jax.ShapeDtypeStruct((group_count, obs_group, AUX), jnp.float32),
+        ),
+        in_specs=[vmem, pl.BlockSpec(memory_space=pl.ANY)],
+        out_specs=(vmem, vmem, vmem),
+        scratch_shapes=[
+            pltpu.VMEM((block_count, structs, width), jnp.float32),
+            pltpu.VMEM((group_count, obs_group, width), jnp.float32),
+            pltpu.VMEM((row_share, order), jnp.float32),
+            pltpu.VMEM((row_share, 128), jnp.float32),
+            pltpu.VMEM((fold, 128), jnp.float32),
+            pltpu.VMEM((near, fold, 128), jnp.float32),
+            pltpu.VMEM((fold, 128), jnp.float32),
+            pltpu.VMEM((far, fold, 128), jnp.float32),
+            dma,
+            dma,
+            dma((2, far)),
+            dma((2, far)),
+            dma((2, near)),
+            dma((2, near)),
+            dma((near,)),
+            dma((near,)),
+            dma((far,)),
+            dma((far,)),
+            dma((near,)),
+            dma((near,)),
+        ],
+        compiler_params=pltpu.CompilerParams(collective_id=0, has_side_effects=True),
+    )(terms, cov_rows)
+
+
+def update_kernel(
+    gram_ref,
+    product_ref,
+    aux_ref,
+    targets_ref,
+    noise_ref,
+    middle_ref,
+    cov_ref,
+    weights_ref,
+    new_cov_ref,
+    gain_ref,
+):
+    step = pl.program_id(0)
+    tile, order = cov_ref.shape
+    row_share = product_ref.shape[2]
+    hidden = middle_ref.shape[1]
+
+    @pl.when(step == 0)
+    def _():
+        row = lax.broadcasted_iota(jnp.int32, (OBS, OBS), 0)
+        column = lax.broadcasted_iota(jnp.int32, (OBS, OBS), 1)
+        gram = gram_ref[...]
+        pad = jnp.zeros((128 - OBS, 128), jnp.float32)
+        flipped = jnp.concatenate([gram, pad], axis=0).T[:OBS]
+        matrix = 0.5 * (gram + flipped)[:, :OBS]
+        matrix = matrix + jnp.where(row == column, noise_ref[...], 0.0)
+        for k in range(OBS):
+            pivot = 1.0 / matrix[k : k + 1, k : k + 1]
+            scaled = jnp.where(column[:1] == k, pivot, matrix[k : k + 1] * pivot)
+            side = jnp.where(row[:, :1] == k, -1.0, matrix[:, k : k + 1])
+            kept = jnp.where(jnp.logical_or(row == k, column == k), 0.0, matrix)
+            matrix = kept - side * scaled
+        group = lax.axis_index("dp")
+        gain = contract(product_ref[group], matrix, 0, 0)
+        gain_ref[...] = gain
+        predicted = jnp.sum(
+            jnp.where(row == column, aux_ref[:, 128 - OBS :], 0.0), axis=0, keepdims=True
+        )
+        innovation = jnp.broadcast_to(targets_ref[...] - predicted, (8, OBS))
+        moved = contract(innovation, gain, 1, 1)[:1]
+        first = lax.axis_index("block") * order + group * row_share
+        for i in range(row_share // 128):
+            flat = first + i * 128
+            line = middle_ref[pl.ds(flat // hidden, 1), :]
+            window = line[:, :128]
+            for j in range(1, hidden // 128):
+                window = jnp.where(
+                    lax.rem(flat, hidden) == j * 128,
+                    line[:, j * 128 : (j + 1) * 128],
+                    window,
+                )
+            here = slice(i * 128, (i + 1) * 128)
+            weights_ref[:, here] = window + moved[:, here]
+
+    gain = gain_ref[pl.ds(pl.multiple_of(step * tile, tile), tile), :]
+    for d in range(product_ref.shape[0]):
+        cols = slice(d * row_share, (d + 1) * row_share)
+        update = contract(gain, product_ref[d], 1, 0)
+        new_cov_ref[:, cols] = (cov_ref[:, cols] - update) * (1.0 / forgetting)
+
+
+def update(gram, product, aux, targets, noise_level, middle_weight, cov_rows):
+    row_share, order = cov_rows.shape
+    tile = min(128, row_share)
+    vmem = pl.BlockSpec(memory_space=pltpu.VMEM)
+    cov_spec = pl.BlockSpec((tile, order), lambda i: (i, 0))
+    return pl.pallas_call(
+        update_kernel,
+        grid=(row_share // tile,),
+        out_shape=(
+            jax.ShapeDtypeStruct((1, row_share), jnp.float32),
+            jax.ShapeDtypeStruct((row_share, order), jnp.float32),
+        ),
+        in_specs=[vmem] * 6 + [cov_spec],
+        out_specs=(pl.BlockSpec((1, row_share), lambda i: (0, 0)), cov_spec),
+        scratch_shapes=[pltpu.VMEM((row_share, OBS), jnp.float32)],
+    )(
+        gram,
+        product,
+        aux.reshape(OBS, AUX),
+        targets[None],
+        noise_level[None],
+        middle_weight,
+        cov_rows,
+    )
+
+
 def local(
     positions,
     neighbours,
@@ -256,10 +557,6 @@
     group_count = lax.axis_size("dp")
     block_count = lax.axis_size("block")
     block_order = covariance.shape[2]
-    row_share = covariance.shape[1]
-    hidden = middle_weight.shape[1]
-    block_rows = block_order // hidden
-    window = middle_weight[: block_rows * block_count]
     obs_group = OBS // group_count
     weighting = OBS / (tagged_atom.shape[0] * group_count * block_count)
     terms = observe(
@@ -279,35 +576,11 @@
         middle_bias,
         energy_weight,
     )
-    chosen = (
-        observed_in[:, None] == jnp.arange(obs_group, dtype=jnp.int32)[None, :]
-    ).astype(jnp.float32)
-    by_obs = jnp.einsum("sq,bsn->bqn", chosen, terms, precision=highest)
-    mine = lax.psum_scatter(by_obs, "block", scatter_dimension=0, tiled=True)[0]
-    everyone = lax.all_gather(mine, "dp", axis=0, tiled=True)
-    jacobian = everyone[:, :block_order]
-    predicted = everyone[:, -1]
-    cov_rows = covariance[0]
-    product = jnp.dot(cov_rows, jacobian.T, precision=highest)
-    columns = lax.dynamic_slice_in_dim(jacobian, lax.axis_index("dp") * row_share, row_share, 1)
-    partial_value = jnp.dot(columns, product, precision=highest)
-    gram_sum = lax.psum(partial_value, ("dp", "block"))
-    gram_sum = 0.5 * (gram_sum + gram_sum.T) + jnp.diag(noise_level)
-    factor = jnp.linalg.cholesky(gram_sum)
-    inverse = jax.scipy.linalg.cho_solve((factor, True), jnp.eye(OBS, dtype=jnp.float32))
-    gain_rows = jnp.dot(product, inverse, precision=highest)
-    product_all = lax.all_gather(product, "dp", axis=0, tiled=True)
-    update = jnp.dot(gain_rows, product_all.T, precision=highest)
-    innovation = targets - predicted
-    block_window = lax.dynamic_slice_in_dim(
-        window.reshape(block_count, block_order), lax.axis_index("block"), 1, 0
-    )
-    window_rows = lax.dynamic_slice_in_dim(
-        block_window, lax.axis_index("dp") * row_share, row_share, 1
-    )
-    new_weights = window_rows + jnp.dot(gain_rows, innovation, precision=highest)[None, :]
-    new_covariance = ((cov_rows - update) / forgetting)[None]
-    return (new_weights, new_covariance)
+    product, gram, aux = exchange(group_count, obs_group, terms, covariance[0])
+    new_weights, new_rows = update(
+        gram, product, aux, targets, noise_level, middle_weight, covariance[0]
+    )
+    return (new_weights, new_rows[None])
 
 
 def solution(mesh):

time: 145 us -> 59.7 us (0.41)
  blocking collectives: 58.8 us -> 0 us
  Pallas kernels: 6.09 us -> 58.7 us
  waiting for transfers between devices: 34.8 us -> 0 us
  matrix products: 17.6 us -> 0 us
  between operations: 14.1 us -> 0.64 us
  other arithmetic: 12.2 us -> 0 us
    pallas_call x0 -> x2, Pallas kernels: none -> 52.6 us  [the longest x1 39 us: exchange(): pl.pallas_call(functools.partial(exchange_kernel, group_count, block_coun...]
    psum x1 -> x0, blocking collectives: 37 us -> none  [local(): gram_sum = lax.psum(partial_value, ('dp', 'block'))]
    reduce_scatter x1 -> x0, waiting for transfers between devices: 34.8 us -> none  [local(): mine = lax.psum_scatter(by_obs, 'block', scatter_dimension=0, tiled=True)[0]]
    all_gather x2 -> x0, blocking collectives: 21.8 us -> none  [the longest x1 11.5 us: local(): product_all = lax.all_gather(product, 'dp', axis=0, tiled=True)]
    dot_general x6 -> x0, matrix products: 17.2 us -> none  [the longest x1 6.78 us: local(): update = jnp.dot(gain_rows, product_all.T, precision=highest)]
    another operation x5 -> x0, other arithmetic: 12.1 us -> none  [the longest x3 6.52 us: local(): factor = jnp.linalg.cholesky(gram_sum)]
  transfers between devices with their start and end apart: 1 -> 0, of which waited for: 1 -> 0; matrix products, arithmetic and copies ran while one was open for 1% -> 0% of each run, Pallas kernels for 0% -> 0%
where the time goes in v2:
time: 59.7 us; the launch traced here: 59.4 us
  Pallas kernels  58.7 us (98%)
  between operations  0.64 us (1%)
    pallas_call x1, Pallas kernels, exchange(): pl.pallas_call(functools.partial(exchange_kernel, group_count, block_coun...  39 us
    pallas_call x1, Pallas kernels, update(): pl.pallas_call(update_kernel, grid=(row_share // tile,), out_shape=(jax.S...  13.7 us
    pallas_call x1, Pallas kernels, observe(): pl.pallas_call(functools.partial(observe_kernel, weighting), out_shape=ja...  6.1 us

profile of v2, /device:TPU:0, one launch (start us, length us, event | category | flops | bytes accessed | tf_op | source)
XLA Modules:
  0.0 59.4 jit_solution(4471395929554345489)
XLA Ops:
  0.6 6.1 %shard_map.158.terms_ref = f32[8,8,2176]{2,1,0:T(8,128)} custom-call(s32[1,8]{1,0:T(1,128)} %bitcast.16, s32[1,8]{1,0:T(1,128)} %bitcast.17, f32[3,256]{1,0:T(4,128)} %positions_ref.1, s32[16,256]{1,0:T(8,128)} %neighbours_ref.1, s32[1,256]{1,0:T(1,128)} %bitcast.13, f32[4,128]{1,0:T(4,128)} %scale_ref.1, f32[4,128]{1,0:T(4,128)} %shift_ref.1, ...), custom_call_target="tpu_custom_call" | custom-call | tf_op jit(solution)/shard_map/pallas_call | solution.py:210
  6.7 39.0 %shard_map.159 = (f32[4,64,512]{2,1,0:T(8,128)}, f32[64,128]{1,0:T(8,128)}, f32[4,16,128]{2,1,0:T(8,128)}) custom-call(f32[8,8,2176]{2,1,0:T(8,128)} %shard_map.158.terms_ref, f32[512,2048]{1,0:T(8,128)} %bitcast.10), custom_call_target="tpu_custom_call" | custom-call | tf_op jit(solution)/shard_map/pallas_call | solution.py:418
  45.7 13.7 %shard_map.160 = (f32[1,512]{1,0:T(1,128)}, f32[512,2048]{1,0:T(8,128)}) custom-call(f32[64,128]{1,0:T(8,128)} %get-tuple-element.7.gram_ref, f32[4,64,512]{2,1,0:T(8,128)} %get-tuple-element.8.product_ref, f32[64,128]{1,0:T(8,128)} %bitcast.12, f32[1,64]{1,0:T(1,128)} %bitcast.18, f32[1,64]{1,0:T(1,128)} %bitcast.19, f32[256,256]{1,0:T(8,128)} %middle_ref.3, ...), custom_call_target="tpu_custom_call" | custom-call | tf_op jit(solution)/shard_map/pallas_call | solution.py:519

commit v3 on v2

--- a/solution.py
+++ b/solution.py
@@ -9,20 +9,32 @@
 
 OBS = 64
 AUX = 128
+CHUNKS = 4
 
 radial_width = 4.0
 forgetting = 0.98
-highest = lax.Precision.HIGHEST
-
-
-def contract(left, right, left_dim, right_dim):
-    return lax.dot_general(
-        left,
-        right,
-        (((left_dim,), (right_dim,)), ((), ())),
-        precision=highest,
-        preferred_element_type=jnp.float32,
-    )
+
+
+def halves(value):
+    high = value.astype(jnp.bfloat16)
+    return high, (value - high.astype(jnp.float32)).astype(jnp.bfloat16)
+
+
+def contract(left, right, left_dim, right_dim, exact_left=False):
+    def one(a, b):
+        return lax.dot_general(
+            a,
+            b,
+            (((left_dim,), (right_dim,)), ((), ())),
+            preferred_element_type=jnp.float32,
+        )
+
+    right_high, right_low = halves(right)
+    left_high, left_low = halves(left)
+    small = one(left_high, right_low)
+    if not exact_left:
+        small = small + one(left_low, right_high)
+    return small + one(left_high, right_high)
 
 
 def observe_kernel(
@@ -273,8 +285,9 @@
     structs, width = terms_ref.shape[1:]
     obs_group = jac.shape[1]
     row_share = cov_ref.shape[0]
-    half = (width - AUX) // 2
-    chunks = ((0, AUX + half), (AUX + half, half))
+    piece = (width - AUX) // CHUNKS
+    chunks = [(0, AUX + piece)]
+    chunks += [(AUX + c * piece, piece) for c in range(1, CHUNKS)]
     group_peers = [(o, lax.rem(group + o, group_count)) for o in range(1, group_count)]
     block_peers = [(o, lax.rem(block + o, block_count)) for o in range(1, block_count)]
 
@@ -330,7 +343,7 @@
             copy.wait_recv()
         chosen = got[:, :, :AUX].reshape(block_count * structs, AUX).T[:obs_group]
         pieces = got[:, :, cols].reshape(block_count * structs, size)
-        jac[group, :, cols] = contract(chosen, pieces, 1, 0)
+        jac[group, :, cols] = contract(chosen, pieces, 1, 0, exact_left=True)
         jac_copies.append(
             [
                 send(
@@ -345,16 +358,14 @@
         )
 
     cov_copy.wait()
-    for c in range(2):
+    for c in range(CHUNKS):
         for copy in jac_copies[c]:
             copy.wait_recv()
-        rows = jac[:, :, AUX + c * half : AUX + (c + 1) * half].reshape(OBS, half)
+        rows = jac[:, :, AUX + c * piece : AUX + (c + 1) * piece].reshape(OBS, piece)
         rows = jnp.concatenate([rows, jnp.zeros_like(rows)], axis=0)
-        part = contract(cov_rows[:, c * half : (c + 1) * half], rows, 1, 1)
-        if c == 0:
-            total[...] = part
-        else:
-            product = (total[...] + part).T
+        part = contract(cov_rows[:, c * piece : (c + 1) * piece], rows, 1, 1)
+        total[...] = part if c == 0 else total[...] + part
+    product = total[...].T
     product_ref[group] = product[:OBS]
     mine = jac[:, :, pl.ds(pl.multiple_of(AUX + group * row_share, 128), row_share)]
     gram = contract(mine.reshape(OBS, row_share), product, 1, 1)
@@ -435,10 +446,10 @@
             pltpu.VMEM((far, fold, 128), jnp.float32),
             dma,
             dma,
-            dma((2, far)),
-            dma((2, far)),
-            dma((2, near)),
-            dma((2, near)),
+            dma((CHUNKS, far)),
+            dma((CHUNKS, far)),
+            dma((CHUNKS, near)),
+            dma((CHUNKS, near)),
             dma((near,)),
             dma((near,)),
             dma((far,)),

time: 59.7 us -> 54.9 us (0.920)
  Pallas kernels: 58.7 us -> 54 us
    pallas_call x1, Pallas kernels: 39 us -> 36.6 us  [exchange(): pl.pallas_call(functools.partial(exchange_kernel, group_count, block_coun...]
    pallas_call x1, Pallas kernels: 13.7 us -> 12.2 us  [update(): pl.pallas_call(update_kernel, grid=(row_share // tile,), out_shape=(jax.S...]
    pallas_call x1, Pallas kernels: 6.1 us -> 5.17 us  [observe(): pl.pallas_call(functools.partial(observe_kernel, weighting), out_shape=ja...]
where the time goes in v3:
time: 54.9 us; the launch traced here: 54.6 us
  Pallas kernels  54 us (98%)
  between operations  0.64 us (1%)
    pallas_call x1, Pallas kernels, exchange(): pl.pallas_call(functools.partial(exchange_kernel, group_count, block_coun...  36.6 us
    pallas_call x1, Pallas kernels, update(): pl.pallas_call(update_kernel, grid=(row_share // tile,), out_shape=(jax.S...  12.2 us
    pallas_call x1, Pallas kernels, observe(): pl.pallas_call(functools.partial(observe_kernel, weighting), out_shape=ja...  5.17 us

profile of v3, /device:TPU:0, one launch (start us, length us, event | category | flops | bytes accessed | tf_op | source)
XLA Modules:
  0.0 54.6 jit_solution(14595000640423474630)
XLA Ops:
  0.6 5.2 %shard_map.158.terms_ref = f32[8,8,2176]{2,1,0:T(8,128)} custom-call(s32[1,8]{1,0:T(1,128)} %bitcast.16, s32[1,8]{1,0:T(1,128)} %bitcast.17, f32[3,256]{1,0:T(4,128)} %positions_ref.1, s32[16,256]{1,0:T(8,128)} %neighbours_ref.1, s32[1,256]{1,0:T(1,128)} %bitcast.13, f32[4,128]{1,0:T(4,128)} %scale_ref.1, f32[4,128]{1,0:T(4,128)} %shift_ref.1, ...), custom_call_target="tpu_custom_call" | custom-call | tf_op jit(solution)/shard_map/pallas_call | solution.py:222
  5.8 36.6 %shard_map.159 = (f32[4,64,512]{2,1,0:T(8,128)}, f32[64,128]{1,0:T(8,128)}, f32[4,16,128]{2,1,0:T(8,128)}) custom-call(f32[8,8,2176]{2,1,0:T(8,128)} %shard_map.158.terms_ref, f32[512,2048]{1,0:T(8,128)} %bitcast.10), custom_call_target="tpu_custom_call" | custom-call | tf_op jit(solution)/shard_map/pallas_call | solution.py:429
  42.4 12.2 %shard_map.160 = (f32[1,512]{1,0:T(1,128)}, f32[512,2048]{1,0:T(8,128)}) custom-call(f32[64,128]{1,0:T(8,128)} %get-tuple-element.7.gram_ref, f32[4,64,512]{2,1,0:T(8,128)} %get-tuple-element.8.product_ref, f32[64,128]{1,0:T(8,128)} %bitcast.12, f32[1,64]{1,0:T(1,128)} %bitcast.18, f32[1,64]{1,0:T(1,128)} %bitcast.19, f32[256,256]{1,0:T(8,128)} %middle_ref.3, ...), custom_call_target="tpu_custom_call" | custom-call | tf_op jit(solution)/shard_map/pallas_call | solution.py:530

commit v4 on v3

--- a/solution.py
+++ b/solution.py
@@ -472,14 +472,18 @@
     weights_ref,
     new_cov_ref,
     gain_ref,
+    cov_rows,
+    cov_sem,
 ):
     step = pl.program_id(0)
-    tile, order = cov_ref.shape
+    tile, order = new_cov_ref.shape
     row_share = product_ref.shape[2]
     hidden = middle_ref.shape[1]
 
     @pl.when(step == 0)
     def _():
+        cov_copy = pltpu.make_async_copy(cov_ref, cov_rows, cov_sem)
+        cov_copy.start()
         row = lax.broadcasted_iota(jnp.int32, (OBS, OBS), 0)
         column = lax.broadcasted_iota(jnp.int32, (OBS, OBS), 1)
         gram = gram_ref[...]
@@ -487,12 +491,26 @@
         flipped = jnp.concatenate([gram, pad], axis=0).T[:OBS]
         matrix = 0.5 * (gram + flipped)[:, :OBS]
         matrix = matrix + jnp.where(row == column, noise_ref[...], 0.0)
-        for k in range(OBS):
-            pivot = 1.0 / matrix[k : k + 1, k : k + 1]
-            scaled = jnp.where(column[:1] == k, pivot, matrix[k : k + 1] * pivot)
-            side = jnp.where(row[:, :1] == k, -1.0, matrix[:, k : k + 1])
-            kept = jnp.where(jnp.logical_or(row == k, column == k), 0.0, matrix)
-            matrix = kept - side * scaled
+        for k in range(0, OBS, 2):
+            upper = matrix[k : k + 1]
+            lower = matrix[k + 1 : k + 2]
+            cross = upper[:, k + 1 : k + 2]
+            first_inverse = 1.0 / upper[:, k : k + 1]
+            ratio = cross * first_inverse
+            last = 1.0 / (lower[:, k + 1 : k + 2] - cross * ratio)
+            mixed = -ratio * last
+            first = first_inverse + ratio * ratio * last
+            place = column[:1]
+            upper_new = jnp.where(place == k, first, first * upper + mixed * lower)
+            upper_new = jnp.where(place == k + 1, mixed, upper_new)
+            lower_new = jnp.where(place == k, mixed, mixed * upper + last * lower)
+            lower_new = jnp.where(place == k + 1, last, lower_new)
+            left = jnp.where(row[:, :1] == k, -1.0, matrix[:, k : k + 1])
+            left = jnp.where(row[:, :1] == k + 1, 0.0, left)
+            right = jnp.where(row[:, :1] == k + 1, -1.0, matrix[:, k + 1 : k + 2])
+            right = jnp.where(row[:, :1] == k, 0.0, right)
+            kept = jnp.where(jnp.logical_or(row >> 1 == k // 2, column >> 1 == k // 2), 0.0, matrix)
+            matrix = kept - left * upper_new - right * lower_new
         group = lax.axis_index("dp")
         gain = contract(product_ref[group], matrix, 0, 0)
         gain_ref[...] = gain
@@ -514,12 +532,14 @@
                 )
             here = slice(i * 128, (i + 1) * 128)
             weights_ref[:, here] = window + moved[:, here]
-
-    gain = gain_ref[pl.ds(pl.multiple_of(step * tile, tile), tile), :]
+        cov_copy.wait()
+
+    rows = pl.ds(pl.multiple_of(step * tile, tile), tile)
+    gain = gain_ref[rows, :]
     for d in range(product_ref.shape[0]):
         cols = slice(d * row_share, (d + 1) * row_share)
         update = contract(gain, product_ref[d], 1, 0)
-        new_cov_ref[:, cols] = (cov_ref[:, cols] - update) * (1.0 / forgetting)
+        new_cov_ref[:, cols] = (cov_rows[rows, cols] - update) * (1.0 / forgetting)
 
 
 def update(gram, product, aux, targets, noise_level, middle_weight, cov_rows):
@@ -534,9 +554,13 @@
             jax.ShapeDtypeStruct((1, row_share), jnp.float32),
             jax.ShapeDtypeStruct((row_share, order), jnp.float32),
         ),
-        in_specs=[vmem] * 6 + [cov_spec],
+        in_specs=[vmem] * 6 + [pl.BlockSpec(memory_space=pl.ANY)],
         out_specs=(pl.BlockSpec((1, row_share), lambda i: (0, 0)), cov_spec),
-        scratch_shapes=[pltpu.VMEM((row_share, OBS), jnp.float32)],
+        scratch_shapes=[
+            pltpu.VMEM((row_share, OBS), jnp.float32),
+            pltpu.VMEM((row_share, order), jnp.float32),
+            pltpu.SemaphoreType.DMA,
+        ],
     )(
         gram,
         product,

time: 54.9 us -> 56 us (1.020)
  Pallas kernels: 54 us -> 55.1 us
    pallas_call x1, Pallas kernels: 12.2 us -> 13.3 us  [update(): pl.pallas_call(update_kernel, grid=(row_share // tile,), out_shape=(jax.S...]
where the time goes in v4:
time: 56 us; the launch traced here: 55.8 us
  Pallas kernels  55.1 us (98%)
  between operations  0.64 us (1%)
    pallas_call x1, Pallas kernels, exchange(): pl.pallas_call(functools.partial(exchange_kernel, group_count, block_coun...  36.6 us
    pallas_call x1, Pallas kernels, update(): pl.pallas_call(update_kernel, grid=(row_share // tile,), out_shape=(jax.S...  13.3 us
    pallas_call x1, Pallas kernels, observe(): pl.pallas_call(functools.partial(observe_kernel, weighting), out_shape=ja...  5.17 us

profile of v4, /device:TPU:0, one launch (start us, length us, event | category | flops | bytes accessed | tf_op | source)
XLA Modules:
  0.0 55.8 jit_solution(12087031531369409325)
XLA Ops:
  0.6 5.2 %shard_map.158.terms_ref = f32[8,8,2176]{2,1,0:T(8,128)} custom-call(s32[1,8]{1,0:T(1,128)} %bitcast.16, s32[1,8]{1,0:T(1,128)} %bitcast.17, f32[3,256]{1,0:T(4,128)} %positions_ref.1, s32[16,256]{1,0:T(8,128)} %neighbours_ref.1, s32[1,256]{1,0:T(1,128)} %bitcast.13, f32[4,128]{1,0:T(4,128)} %scale_ref.1, f32[4,128]{1,0:T(4,128)} %shift_ref.1, ...), custom_call_target="tpu_custom_call" | custom-call | tf_op jit(solution)/shard_map/pallas_call | solution.py:222
  5.8 36.6 %shard_map.159 = (f32[4,64,512]{2,1,0:T(8,128)}, f32[64,128]{1,0:T(8,128)}, f32[4,16,128]{2,1,0:T(8,128)}) custom-call(f32[8,8,2176]{2,1,0:T(8,128)} %shard_map.158.terms_ref, f32[512,2048]{1,0:T(8,128)} %bitcast.10), custom_call_target="tpu_custom_call" | custom-call | tf_op jit(solution)/shard_map/pallas_call | solution.py:429
  42.4 13.3 %shard_map.160 = (f32[1,512]{1,0:T(1,128)}, f32[512,2048]{1,0:T(8,128)}) custom-call(f32[64,128]{1,0:T(8,128)} %get-tuple-element.7.gram_ref, f32[4,64,512]{2,1,0:T(8,128)} %get-tuple-element.8.product_ref, f32[64,128]{1,0:T(8,128)} %bitcast.12, f32[1,64]{1,0:T(1,128)} %bitcast.18, f32[1,64]{1,0:T(1,128)} %bitcast.19, f32[256,256]{1,0:T(8,128)} %middle_ref.3, ...), custom_call_target="tpu_custom_call" | custom-call | tf_op jit(solution)/shard_map/pallas_call | solution.py:550

commit v5 on v3

--- a/solution.py
+++ b/solution.py
@@ -472,14 +472,18 @@
     weights_ref,
     new_cov_ref,
     gain_ref,
+    cov_rows,
+    cov_sem,
 ):
     step = pl.program_id(0)
-    tile, order = cov_ref.shape
+    tile, order = new_cov_ref.shape
     row_share = product_ref.shape[2]
     hidden = middle_ref.shape[1]
 
     @pl.when(step == 0)
     def _():
+        cov_copy = pltpu.make_async_copy(cov_ref, cov_rows, cov_sem)
+        cov_copy.start()
         row = lax.broadcasted_iota(jnp.int32, (OBS, OBS), 0)
         column = lax.broadcasted_iota(jnp.int32, (OBS, OBS), 1)
         gram = gram_ref[...]
@@ -514,12 +518,14 @@
                 )
             here = slice(i * 128, (i + 1) * 128)
             weights_ref[:, here] = window + moved[:, here]
-
-    gain = gain_ref[pl.ds(pl.multiple_of(step * tile, tile), tile), :]
+        cov_copy.wait()
+
+    rows = pl.ds(pl.multiple_of(step * tile, tile), tile)
+    gain = gain_ref[rows, :]
     for d in range(product_ref.shape[0]):
         cols = slice(d * row_share, (d + 1) * row_share)
         update = contract(gain, product_ref[d], 1, 0)
-        new_cov_ref[:, cols] = (cov_ref[:, cols] - update) * (1.0 / forgetting)
+        new_cov_ref[:, cols] = (cov_rows[rows, cols] - update) * (1.0 / forgetting)
 
 
 def update(gram, product, aux, targets, noise_level, middle_weight, cov_rows):
@@ -534,9 +540,13 @@
             jax.ShapeDtypeStruct((1, row_share), jnp.float32),
             jax.ShapeDtypeStruct((row_share, order), jnp.float32),
         ),
-        in_specs=[vmem] * 6 + [cov_spec],
+        in_specs=[vmem] * 6 + [pl.BlockSpec(memory_space=pl.ANY)],
         out_specs=(pl.BlockSpec((1, row_share), lambda i: (0, 0)), cov_spec),
-        scratch_shapes=[pltpu.VMEM((row_share, OBS), jnp.float32)],
+        scratch_shapes=[
+            pltpu.VMEM((row_share, OBS), jnp.float32),
+            pltpu.VMEM((row_share, order), jnp.float32),
+            pltpu.SemaphoreType.DMA,
+        ],
     )(
         gram,
         product,

time: 54.9 us -> 53.6 us (0.976)
  Pallas kernels: 54 us -> 52.7 us
    pallas_call x1, Pallas kernels: 12.2 us -> 10.9 us  [update(): pl.pallas_call(update_kernel, grid=(row_share // tile,), out_shape=(jax.S...]
where the time goes in v5:
time: 53.6 us; the launch traced here: 53.4 us
  Pallas kernels  52.7 us (98%)
  between operations  0.64 us (1%)
    pallas_call x1, Pallas kernels, exchange(): pl.pallas_call(functools.partial(exchange_kernel, group_count, block_coun...  36.6 us
    pallas_call x1, Pallas kernels, update(): pl.pallas_call(update_kernel, grid=(row_share // tile,), out_shape=(jax.S...  10.9 us
    pallas_call x1, Pallas kernels, observe(): pl.pallas_call(functools.partial(observe_kernel, weighting), out_shape=ja...  5.17 us

profile of v5, /device:TPU:0, one launch (start us, length us, event | category | flops | bytes accessed | tf_op | source)
XLA Modules:
  0.0 53.4 jit_solution(5680730293964493151)
XLA Ops:
  0.6 5.2 %shard_map.158.terms_ref = f32[8,8,2176]{2,1,0:T(8,128)} custom-call(s32[1,8]{1,0:T(1,128)} %bitcast.16, s32[1,8]{1,0:T(1,128)} %bitcast.17, f32[3,256]{1,0:T(4,128)} %positions_ref.1, s32[16,256]{1,0:T(8,128)} %neighbours_ref.1, s32[1,256]{1,0:T(1,128)} %bitcast.13, f32[4,128]{1,0:T(4,128)} %scale_ref.1, f32[4,128]{1,0:T(4,128)} %shift_ref.1, ...), custom_call_target="tpu_custom_call" | custom-call | tf_op jit(solution)/shard_map/pallas_call | solution.py:222
  5.8 36.6 %shard_map.159 = (f32[4,64,512]{2,1,0:T(8,128)}, f32[64,128]{1,0:T(8,128)}, f32[4,16,128]{2,1,0:T(8,128)}) custom-call(f32[8,8,2176]{2,1,0:T(8,128)} %shard_map.158.terms_ref, f32[512,2048]{1,0:T(8,128)} %bitcast.10), custom_call_target="tpu_custom_call" | custom-call | tf_op jit(solution)/shard_map/pallas_call | solution.py:429
  42.4 10.9 %shard_map.160 = (f32[1,512]{1,0:T(1,128)}, f32[512,2048]{1,0:T(8,128)}) custom-call(f32[64,128]{1,0:T(8,128)} %get-tuple-element.7.gram_ref, f32[4,64,512]{2,1,0:T(8,128)} %get-tuple-element.8.product_ref, f32[64,128]{1,0:T(8,128)} %bitcast.12, f32[1,64]{1,0:T(1,128)} %bitcast.18, f32[1,64]{1,0:T(1,128)} %bitcast.19, f32[256,256]{1,0:T(8,128)} %middle_ref.3, ...), custom_call_target="tpu_custom_call" | custom-call | tf_op jit(solution)/shard_map/pallas_call | solution.py:536
